TPU v7x, 256 devices: a whole 4x4x8 slice. The times are simulated.
256 devices in a mesh: lon: 16 (over y, x), lat: 8 (over z), mem: 2 (over core).
Axes of the slice: x: 4, y: 4, z: 8, core: 2. Of those that a mesh axis runs over, the one named last changes fastest.
Arguments:
- anomalies: bfloat16 [128, 128, 4096], P('mem', 'lat', 'lon'), may hold values from -6 to 6
- state_mean: float32 [128, 4096], P('lat', 'lon'), may hold values from -6 to 6
- delayed_deviation_pair: bfloat16 [2, 128, 128, 4096], P(None, 'mem', 'lat', 'lon'), may hold values from -6 to 6
- lagged_means: float32 [2, 128, 4096], P(None, 'lat', 'lon'), may hold values from -6 to 6
- courant_lon: float32 [128, 4096], P('lat', 'lon'), may hold values from -0.45 to 0.45
- courant_lat: float32 [128, 4096], P('lat', 'lon'), may hold values from -0.45 to 0.45
- ocean: int32 [128, 4096], P('lat', 'lon'), may hold values 0 or 1
- obs_values: float32 [16384, 64], P(('lon', 'lat')), may hold values from -160 to 160
- obs_variance: float32 [16384, 64], P(('lon', 'lat')), may hold values from 2048 to 32768
- obs_cells: int32 [16384, 64], P(('lon', 'lat')), may hold values from 0 to 4095
- obs_tile: int32 [16384, 1], P(('lon', 'lat')), may hold values from 0 to 127; in each aligned block of 128 rows (0 to 127, 128 to 255, ...) at most 2 rows name the same one
- obs_count: int32 [16384], P(('lon', 'lat')), may hold values from 48 to 64
Outputs:
- analysis_anomalies: bfloat16 [3, 128, 128, 4096], P(None, 'mem', 'lat', 'lon')
- analysis_mean: float32 [3, 128, 4096], P(None, 'lat', 'lon')
Inputs may be any that keep to these rules, and one draw needn't show every extreme that they name: `obs_tile`: among the 128 blocks of one tile (an aligned run of rows) no tile is named more than 2 times.
All inputs are finite; a program needn't handle non-finite values. Where the computation divides by a largest or mean magnitude, that divisor is 1e-20 or more. No bound on the sum of `ocean` on one device may be relied on, other than what follows from the above.
Results may differ from a plain program's by a relative error of at most 0.0034.
Values may be sent and summed in bfloat16 or wider, within the bound.
A program may use at most 64 MiB of HBM per device.

v0:
```python
import math
import jax
import jax.numpy as jnp
from jax import lax
from jax.sharding import Mesh
from jax.sharding import PartitionSpec as P

SUBSTEPS = 4
NS_ITERS = 8
LON = ("lon_0", "lon_1")
LON_LAT = ("lon_0", "lon_1", "lat")


def with_halo(x, sides, width, wrap):
    for axis, dim in sides:
        count, length = (lax.axis_size(axis), x.shape[dim])
        up = [(i, (i + 1) % count) for i in range(count if wrap else count - 1)]
        down = [(j, i) for i, j in up]
        last = lax.slice_in_dim(x, length - width, length, axis=dim)
        leading = lax.slice_in_dim(x, 0, width, axis=dim)
        before = lax.ppermute(last, axis, up)
        after = lax.ppermute(leading, axis, down)
        x = jnp.concatenate([before, x, after], axis=dim)
    return x


def sent_together(arrays, axis, split_dim, concat_dim, along):
    widths = [a.shape[along] for a in arrays]
    both = jnp.concatenate(arrays, axis=along)
    out = lax.all_to_all(both, axis, split_axis=split_dim, concat_axis=concat_dim, tiled=True)
    return tuple(jnp.split(out, [sum(widths[:k]) for k in range(1, len(widths))], axis=along))


def over_axes(x, axes):
    for axis in axes:
        x = lax.psum(x, axis)
    return x


def side_by_side(arrays, axis, dim, along):
    widths = [math.prod(a.shape[along:]) for a in arrays]
    both = jnp.concatenate(
        [a.reshape(*a.shape[:along], w) for a, w in zip(arrays, widths)], axis=along
    )
    out = lax.all_gather(both, axis, axis=dim, tiled=True)
    blocks = jnp.split(out, [sum(widths[:k]) for k in range(1, len(widths))], axis=along)
    return tuple((b.reshape(*out.shape[:along], *a.shape[along:]) for a, b in zip(arrays, blocks)))


def upwind(center, western, eastern, southern, northern, courant_x, courant_y, wet_mask):
    tendency = (
        jnp.maximum(courant_x, 0.0) * (center - western)
        + jnp.minimum(courant_x, 0.0) * (eastern - center)
        + jnp.maximum(courant_y, 0.0) * (center - southern)
        + jnp.minimum(courant_y, 0.0) * (northern - center)
    )
    return center - wet_mask * tendency


def inverse_root(gram, projection):
    members = gram.shape[0]
    identity = jnp.eye(members, dtype=jnp.float32)
    system = (members - 1.0) * identity + 0.5 * (gram + gram.T)
    bound = jnp.max(jnp.sum(jnp.abs(system), axis=1))
    iterate = system / bound
    accum = identity
    for sweep in range(NS_ITERS):
        factor = 1.5 * identity - 0.5 * jnp.dot(accum, iterate, precision=lax.Precision.HIGHEST)
        iterate = jnp.dot(iterate, factor, precision=lax.Precision.HIGHEST)
        accum = jnp.dot(factor, accum, precision=lax.Precision.HIGHEST)
    root = accum / jnp.sqrt(bound)
    weights = jnp.dot(
        root,
        jnp.dot(root, projection, precision=lax.Precision.HIGHEST),
        precision=lax.Precision.HIGHEST,
    )
    transform = jnp.sqrt(members - 1.0) * root
    return (transform.astype(jnp.bfloat16), weights.astype(jnp.bfloat16))


def body(
    anomalies,
    state_mean,
    delayed_deviation_pair,
    lagged_means,
    courant_lon,
    courant_lat,
    ocean,
    obs_values,
    obs_variance,
    obs_cells,
    obs_tile,
    obs_count,
):
    locally_held_samples = anomalies.shape[0]
    wet_mask = ocean.astype(jnp.float32)
    coefficients = jnp.stack([courant_lon, courant_lat, wet_mask])
    sample_surfaces = jnp.concatenate([anomalies.astype(jnp.float32), state_mean[None]], 0)
    stacked = jnp.concatenate([sample_surfaces, coefficients], 0)
    widened = with_halo(stacked, ((LON, 2),), SUBSTEPS, True)
    extended = with_halo(widened.astype(jnp.bfloat16), (("lat", 1),), SUBSTEPS, False).astype(
        widened.dtype
    )
    field_count = sample_surfaces.shape[0]
    sample_surfaces = extended[:field_count]
    beside_all = extended[field_count:]
    for substep in range(SUBSTEPS):
        inner = beside_all[
            :,
            substep + 1 : beside_all.shape[1] - substep - 1,
            substep + 1 : beside_all.shape[2] - substep - 1,
        ]
        sample_surfaces = upwind(
            sample_surfaces[:, 1:-1, 1:-1],
            sample_surfaces[:, 1:-1, :-2],
            sample_surfaces[:, 1:-1, 2:],
            sample_surfaces[:, :-2, 1:-1],
            sample_surfaces[:, 2:, 1:-1],
            inner[0],
            inner[1],
            inner[2],
        )
    predicted_sample_vectors = sample_surfaces[:locally_held_samples].astype(jnp.bfloat16)
    prior_mean = sample_surfaces[locally_held_samples]
    total_cells = prior_mean.shape[0] * prior_mean.shape[1]
    tiles = lax.axis_size(LON_LAT)
    block_total = obs_values.shape[0]
    slot_width = obs_values.shape[1]
    capacity = 2 * block_total // tiles
    target = obs_tile[:, 0]
    block_order = jnp.arange(block_total, dtype=jnp.int32)
    same_target = target[:, None] == target[None, :]
    earlier = block_order[:, None] > block_order[None, :]
    position = jnp.sum((same_target & earlier).astype(jnp.int32), 1)
    destination = target * capacity + position
    placement_table = (
        destination[:, None] == jnp.arange(tiles * capacity, dtype=jnp.int32)[None, :]
    ).astype(jnp.float32)
    valid = jnp.arange(slot_width, dtype=jnp.int32)[None, :] < obs_count[:, None]
    weight = jnp.where(valid, 1.0 / obs_variance, 0.0)
    packed = jnp.concatenate([obs_values, weight, obs_cells.astype(jnp.float32)], 1)
    placed = lax.dot_general(
        placement_table, packed, (((0,), (0,)), ((), ())), precision=lax.Precision.HIGHEST
    ).reshape(tiles, capacity, 3, slot_width)
    arrived_values = sent_together(
        (placed[:, :, 0], placed[:, :, 1], placed[:, :, 2]), LON_LAT, 0, 0, 1
    )
    grid_cells = arrived_values[2].reshape(-1).astype(jnp.int32)
    obs_weight = arrived_values[1].reshape(-1)
    scaled_value = obs_weight * arrived_values[0].reshape(-1)
    rows, columns = (prior_mean.shape[0], prior_mean.shape[1])
    planes = []
    for plane in (obs_weight, scaled_value):
        upper = plane.astype(jnp.bfloat16)
        planes += [upper, (plane - upper.astype(jnp.float32)).astype(jnp.bfloat16)]
    in_row = (grid_cells // columns)[None, :] == jnp.arange(rows, dtype=jnp.int32)[:, None]
    in_column = (grid_cells % columns)[None, :] == jnp.arange(columns, dtype=jnp.int32)[:, None]
    spread = jnp.concatenate(
        [jnp.where(in_row, p[None, :], jnp.zeros((), jnp.bfloat16)) for p in planes], 0
    )
    sums = lax.dot_general(
        spread,
        in_column.astype(jnp.bfloat16),
        (((1,), (1,)), ((), ())),
        preferred_element_type=jnp.float32,
    ).reshape(2, 2, rows, columns)
    cell_weight = sums[0, 0] + sums[0, 1]
    cell_misfit = sums[1, 0] + sums[1, 1] - cell_weight * prior_mean
    observed = predicted_sample_vectors.reshape(locally_held_samples, total_cells)
    weighted = (observed.astype(jnp.float32) * cell_weight.reshape(-1)).astype(jnp.bfloat16)
    observed_all = lax.all_gather(observed, "mem", axis=0, tiled=True)
    gram_part = lax.dot_general(
        weighted, observed_all, (((1,), (1,)), ((), ())), preferred_element_type=jnp.float32
    )
    projection_part = lax.dot_general(
        observed,
        cell_misfit.reshape(-1).astype(jnp.bfloat16),
        (((1,), (0,)), ((), ())),
        preferred_element_type=jnp.float32,
    )
    gram_part, projection_part = (
        over_axes(gram_part, LON_LAT),
        over_axes(projection_part, LON_LAT),
    )
    gram, projection = side_by_side((gram_part, projection_part), "mem", 0, 1)
    transform, weights = inverse_root(gram, projection)
    marine_sample_vectors = jnp.concatenate(
        [predicted_sample_vectors[None], delayed_deviation_pair], 0
    )
    flat_states = marine_sample_vectors.reshape(3, locally_held_samples, total_cells)
    first_member = lax.axis_index("mem") * locally_held_samples
    own_columns = lax.dynamic_slice_in_dim(transform, first_member, locally_held_samples, 1)
    segment = lax.all_gather(marine_sample_vectors, "mem", axis=1, tiled=True)
    length = segment.shape[1]
    flat_segment = segment.reshape(3, length, total_cells)
    moved_sum = jnp.einsum(
        "nk,snc->skc", own_columns, flat_segment, preferred_element_type=jnp.float32
    )
    increment_sum = jnp.einsum(
        "n,snc->sc", weights, flat_segment, preferred_element_type=jnp.float32
    )
    wet_flat = wet_mask.reshape(-1)
    states_float = flat_states.astype(jnp.float32)
    blended = (states_float + wet_flat * (moved_sum - states_float)).astype(jnp.bfloat16)
    analysis_anomalies = blended.reshape(marine_sample_vectors.shape)
    state_means = jnp.concatenate([prior_mean[None], lagged_means], 0)
    analysis_mean = state_means + wet_mask * increment_sum.reshape(state_means.shape)
    return (analysis_anomalies, analysis_mean)


def solution(mesh):
    finer = Mesh(
        mesh.devices.reshape(4, 4, mesh.shape["lat"], mesh.shape["mem"]),
        ("lon_0", "lon_1", "lat", "mem"),
    )
    return jax.shard_map(
        body,
        mesh=finer,
        in_specs=(
            P("mem", "lat", LON),
            P("lat", LON),
            P(None, "mem", "lat", LON),
            P(None, "lat", LON),
            P("lat", LON),
            P("lat", LON),
            P("lat", LON),
            P(LON_LAT, None),
            P(LON_LAT, None),
            P(LON_LAT, None),
            P(LON_LAT, None),
            P(LON_LAT),
        ),
        out_specs=(P(None, "mem", "lat", LON), P(None, "lat", LON)),
        check_vma=False,
    )
```

profile of v0, /device:TPU:1, one launch (start us, length us, event | category | flops | bytes accessed | tf_op | source)
XLA Modules:
  0.0 169.0 jit_solution(13560718712493647950)
XLA Ops:
  7.2 1.1 convert_dynamic-update-slice_fusion
  8.3 0.7 bitcast_dynamic-update-slice_fusion.3
  9.1 0.7 bitcast_dynamic-update-slice_fusion.2
  9.8 0.7 bitcast_dynamic-update-slice_fusion.1
  10.5 0.7 bitcast_dynamic-update-slice_fusion
  11.4 0.3 copy.67
  11.7 2.1 %collective-permute-start = (bf16[68,16,4]{0,1,2:T(8,128)(2,1)S(1)}, bf16[68,16,4]{0,1,2:T(8,128)(2,1)S(1)}, u32[]{:S(2)}, u32[]{:S(2)}) collective-permute-start(bf16[68,16,4]{0,1,2:T(8,128)(2,1)S(1)} %copy.67), channel_id=1, source_target_pairs={{0,16},{16,32},{32,48},{48,64},{64,80},{80,96},{96,112},{112,128},... | collective-permute-start | bytes 26120 | tf_op jit(solution)/shard_map/ppermute | solution.py:21
  13.8 0.3 copy.68
  14.1 3.8 %collective-permute-start.1 = (bf16[68,16,4]{0,1,2:T(8,128)(2,1)S(1)}, bf16[68,16,4]{0,1,2:T(8,128)(2,1)S(1)}, u32[]{:S(2)}, u32[]{:S(2)}) collective-permute-start(bf16[68,16,4]{0,1,2:T(8,128)(2,1)S(1)} %copy.68), channel_id=1, source_target_pairs={{16,0},{32,16},{48,32},{64,48},{80,64},{96,80},{112,96},{128,112},... | collective-permute-start | bytes 26120 | tf_op jit(solution)/shard_map/ppermute | solution.py:22
  18.1 0.5 collective-permute-done
  18.6 0.3 copy.69
  19.0 0.3 copy.70
  19.3 0.6 pad_maximum_fusion.4
  19.9 3.6 %collective-permute-start.2 = (bf16[68,4,264]{2,1,0:T(4,128)(2,1)S(1)}, bf16[68,4,264]{2,1,0:T(4,128)(2,1)S(1)}, u32[]{:S(2)}, u32[]{:S(2)}) collective-permute-start(bf16[68,4,264]{2,1,0:T(4,128)(2,1)S(1)} %get-tuple-element.34), channel_id=1, source_target_pairs={{0,2},{2,4},{4,6},{6,8},{8,10},{10,12},{12,14},{1,3},{3,5},{5,7},{... | collective-permute-start | bytes 430856 | tf_op jit(solution)/shard_map/ppermute | solution.py:21
  23.5 1.5 collective-permute-start.3
  24.9 1.2 collective-permute-done.2
  26.2 4.0 %collective-permute-done.3 = bf16[68,4,264]{2,1,0:T(4,128)(2,1)S(1)} collective-permute-done((bf16[68,4,264]{2,1,0:T(4,128)(2,1)S(1)}, bf16[68,4,264]{2,1,0:T(4,128)(2,1)S(1)}, u32[]{:S(2)}, u32[]{:S(2)}) %collective-permute-start.3) | collective-permute-done | bytes 143648 | tf_op jit(solution)/shard_map/ppermute | solution.py:22
  30.7 1.3 maximum_convert_fusion
  32.0 2.6 %fusion.30 = f32[65,22,262]{2,1,0:T(8,128)S(1)} fusion(f32[68,24,264]{2,1,0:T(8,128)S(1)} %maximum_convert_fusion, f32[22,262]{1,0:T(8,128)S(1)} %get-tuple-element.59, f32[22,262]{1,0:T(8,128)S(1)} %get-tuple-element.32, f32[22,262]{1,0:T(8,128)S(1)} %get-tuple-element.58, f32[22,262]{1,0:T(8,128)S(1)} %get-tuple-element.22, ...), kind=kLoop, calls=%fused_computation.41 | loop fusion | flops 4870580 | bytes 9107120 | tf_op jit(solution)/shard_map/sub | solution.py:57
  34.7 2.6 %fusion.21 = f32[65,20,260]{2,1,0:T(8,128)S(1)} fusion(f32[65,22,262]{2,1,0:T(8,128)S(1)} %fusion.30, f32[20,260]{1,0:T(8,128)S(1)} %get-tuple-element.61, f32[20,260]{1,0:T(8,128)S(1)} %get-tuple-element.30, f32[20,260]{1,0:T(8,128)S(1)} %get-tuple-element.60, f32[20,260]{1,0:T(8,128)S(1)} %get-tuple-element.18, f32[20,260]{1,0:T(8,128)S(1)} %convert_bitcast_fusion.1), kind=kLoop, calls=%fused_computation.28 | loop fusion | flops 4394000 | bytes 8216000 | tf_op jit(solution)/shard_map/sub | solution.py:57
  37.4 2.6 %fusion.12 = f32[65,18,258]{2,1,0:T(8,128)S(1)} fusion(f32[65,20,260]{2,1,0:T(8,128)S(1)} %fusion.21, f32[18,258]{1,0:T(8,128)S(1)} %get-tuple-element.63, f32[18,258]{1,0:T(8,128)S(1)} %get-tuple-element.28, f32[18,258]{1,0:T(8,128)S(1)} %get-tuple-element.62, f32[18,258]{1,0:T(8,128)S(1)} %get-tuple-element.14, f32[18,258]{1,0:T(8,128)S(1)} %convert_bitcast_fusion), kind=kLoop, calls=%fused_computation.15 | loop fusion | flops 3924180 | bytes 7337520 | tf_op jit(solution)/shard_map/sub | solution.py:57
  40.1 1.2 fusion.56
  41.3 1.0 copy.84
  42.4 0.4 fusion.69
  43.0 0.3 fusion.118
  43.3 0.4 pad_maximum_fusion.1
  43.8 0.9 reshape.150
  44.7 14.7 %all-to-all-start = ((f32[128,1,384]{2,1,0:T(1,128)}), f32[128,1,384]{2,1,0:T(1,128)S(1)}, u32[]{:S(2)}, u32[]{:S(2)}) async-start(f32[128,1,384]{2,1,0:T(1,128)} %reshape.150), calls=%async_computation | async-start | bytes 393216 | tf_op jit(solution)/shard_map/all_to_all | solution.py:30
  59.5 1.3 concatenate.39
  60.8 1.0 concatenate.38
  61.9 1.3 pad_maximum_fusion
  63.2 8.0 %all-to-all-done = f32[128,1,384]{2,1,0:T(1,128)S(1)} async-done(((f32[128,1,384]{2,1,0:T(1,128)}), f32[128,1,384]{2,1,0:T(1,128)S(1)}, u32[]{:S(2)}, u32[]{:S(2)}) %all-to-all-start) | async-done | bytes 196640 | tf_op jit(solution)/shard_map/all_to_all | solution.py:30
  71.1 0.5 broadcast.165
  71.7 1.1 reduce.2
  73.5 0.3 fusion.65
  73.9 3.0 %fusion = f32[64,256]{1,0:T(8,128)S(1)} fusion(s32[16384]{0:T(1024)S(1)} %get-tuple-element.55, bf16[16,16384]{1,0:T(8,128)(2,1)S(1)} %get-tuple-element.49, bf16[16,16384]{1,0:T(8,128)(2,1)S(1)} %get-tuple-element.50, bf16[16,16384]{1,0:T(8,128)(2,1)S(1)} %get-tuple-element.51, bf16[16,16384]{1,0:T(8,128)(2,1)S(1)} %get-tuple-element.48), kind=kOutput, calls=%fused_computation.1 | convolution fusion | flops 549453824 | bytes 2228224 | tf_op jit(solution)/shard_map/dot_general | solution.py:161
  76.9 0.2 convolution_bitcast_fusion.3
  77.2 1.7 %fusion.66 = f32[64,128]{1,0:T(8,128)S(1)} fusion(bf16[128,4096]{1,0:T(8,128)(2,1)} %all-gather.5.cloned.1.call-done, bf16[64,4096]{1,0:T(8,128)(2,1)S(1)} %bitcast.200, f32[4096]{0:T(1024)S(1)} %bitcast.207), kind=kOutput, calls=%fused_computation.102 | convolution fusion | flops 67895296 | bytes 1622016 | tf_op jit(solution)/shard_map/dot_general | solution.py:172
  78.9 11.4 %all-reduce.2 = (f32[64]{0:T(128)S(1)}, f32[64,128]{1,0:T(8,128)S(1)}) all-reduce(f32[64]{0:T(128)S(1)} %convolution_bitcast_fusion.3, f32[64,128]{1,0:T(8,128)S(1)} %fusion.66), channel_id=1, replica_groups=mesh['lon_0'=4,'lon_1'=4,'lat'=8,'mem'=2] {'lon_0'}, use_global_device_ids=true, to_apply=%region_4.5 | all-reduce | flops 8256 | bytes 66048 | tf_op jit(solution)/shard_map/psum | solution.py:36
  90.3 11.9 %all-reduce.1 = (f32[64]{0:T(128)S(1)}, f32[64,128]{1,0:T(8,128)S(1)}) all-reduce(f32[64]{0:T(128)S(1)} %get-tuple-element.6, f32[64,128]{1,0:T(8,128)S(1)} %get-tuple-element.7), channel_id=1, replica_groups=mesh['lon_0'=4,'lon_1'=4,'lat'=8,'mem'=2] {'lon_1'}, use_global_device_ids=true, to_apply=%region_5.6 | all-reduce | flops 8256 | bytes 66048 | tf_op jit(solution)/shard_map/psum | solution.py:36
  102.4 21.2 %all-reduce = (f32[64,1]{1,0:T(8,128)S(1)}, f32[64,128]{1,0:T(8,128)S(1)}) all-reduce(f32[64,1]{1,0:T(8,128)S(1)} %copy.74, f32[64,128]{1,0:T(8,128)S(1)} %get-tuple-element.5), channel_id=1, replica_groups=mesh['lon_0'=4,'lon_1'=4,'lat'=8,'mem'=2] {'lat'}, use_global_device_ids=true, to_apply=%region_6.7 | all-reduce | flops 8256 | bytes 66048 | tf_op jit(solution)/shard_map/psum | solution.py:36
  123.6 21.1 %all_gather.11 = f32[128,129]{1,0:T(8,128)S(1)} all-gather(f32[64,129]{1,0:T(8,128)S(1)} %pad_maximum_fusion.5), channel_id=1, replica_groups=mesh['lon_0'=4,'lon_1'=4,'lat'=8,'mem'=2] {'mem'}, dimensions={0}, use_global_device_ids=true | all-gather | bytes 99072 | tf_op jit(solution)/shard_map/all_gather | solution.py:45
  144.9 0.6 reduce_max.9
  145.5 0.8 fusion.50
  146.4 0.9 fusion.96
  147.4 0.2 fusion.49
  148.0 0.2 fusion.48
  148.5 0.2 fusion.122
  148.7 0.2 fusion.47
  148.9 0.2 fusion.125
  149.9 0.2 fusion.124
  150.1 0.2 fusion.46
  150.3 0.2 fusion.127
  150.5 0.2 fusion.126
  150.8 0.2 fusion.45
  151.2 0.2 fusion.128
  151.4 0.2 fusion.44
  152.0 0.2 fusion.43
  152.2 0.3 convolution_divide_fusion
  152.9 4.2 %reshape.129 = bf16[3,128,4096]{2,1,0:T(8,128)(2,1)S(1)} reshape(bf16[3,128,16,256]{3,2,1,0:T(8,128)(2,1)} %all-gather.3.cloned.1.call-done) | data formatting | bytes 6291456 | tf_op jit(solution)/shard_map/reshape | solution.py:195
  157.1 2.3 %fusion.5 = bf16[3,64,4096]{2,1,0:T(8,128)(2,1)S(1)} fusion(bf16[3,128,4096]{2,1,0:T(8,128)(2,1)S(1)} %reshape.129, bf16[2,64,4096]{2,1,0:T(8,128)(2,1)} %concatenate.39, bf16[1,64,4096]{2,1,0:T(8,128)(2,1)} %concatenate.38, f32[4096]{0:T(1024)S(1)} %bitcast.210, f32[128,128]{0,1:T(8,128)S(1)} %convolution_divide_fusion, s32[]{:T(128)S(6)} %select_n.47), kind=kOutput, calls=%fused_computation.7 | convolution fusion | flops 206061568 | bytes 6340612 | tf_op jit(solution)/shard_map/nk,snc->skc/dot_general | solution.py:196
  159.4 1.6 copy.87
  161.0 0.5 fusion.6
  161.5 0.6 maximum_add_fusion
  (76 shorter events, 4.5 us)
Async XLA Ops:
  7.2 10.8 %copy-start.5 = (f32[128,64]{0,1:T(8,128)S(1)}, f32[128,64]{0,1:T(8,128)}, u32[]{:S(2)}) copy-start(f32[128,64]{0,1:T(8,128)} %param.20) | copy-start | bytes 98308
  7.2 10.7 %copy-start.8 = (s32[128]{0:T(128)S(1)}, s32[128]{0:T(128)}, u32[]{:S(2)}) copy-start(s32[128]{0:T(128)} %param.23) | copy-start | bytes 1540
  7.2 10.8 %copy-start.9 = (s32[128,1]{0,1:T(1,128)S(1)}, s32[128,1]{0,1:T(1,128)}, u32[]{:S(2)}) copy-start(s32[128,1]{0,1:T(1,128)} %param.22) | copy-start | bytes 1540
  7.2 10.9 %copy-start.6 = (s32[128,64]{0,1:T(8,128)S(1)}, s32[128,64]{0,1:T(8,128)}, u32[]{:S(2)}) copy-start(s32[128,64]{0,1:T(8,128)} %param.21) | copy-start | bytes 98308
  7.2 70.0 %all-gather.5.cloned.1.call-start = ((), (), s32[]{:S(2)}) async-start(), calls=%async_computation.2 | async-start | bytes 1572864 | tf_op jit(solution)/shard_map/all_gather | solution.py:171
  11.7 6.9 %collective-permute-start = (bf16[68,16,4]{0,1,2:T(8,128)(2,1)S(1)}, bf16[68,16,4]{0,1,2:T(8,128)(2,1)S(1)}, u32[]{:S(2)}, u32[]{:S(2)}) collective-permute-start(bf16[68,16,4]{0,1,2:T(8,128)(2,1)S(1)} %copy.67), channel_id=1, source_target_pairs={{0,16},{16,32},{32,48},{48,64},{64,80},{80,96},{96,112},{112,128},... | collective-permute-start | bytes 26120 | tf_op jit(solution)/shard_map/ppermute | solution.py:21
  14.1 4.8 %collective-permute-start.1 = (bf16[68,16,4]{0,1,2:T(8,128)(2,1)S(1)}, bf16[68,16,4]{0,1,2:T(8,128)(2,1)S(1)}, u32[]{:S(2)}, u32[]{:S(2)}) collective-permute-start(bf16[68,16,4]{0,1,2:T(8,128)(2,1)S(1)} %copy.68), channel_id=1, source_target_pairs={{16,0},{32,16},{48,32},{64,48},{80,64},{96,80},{112,96},{128,112},... | collective-permute-start | bytes 26120 | tf_op jit(solution)/shard_map/ppermute | solution.py:22
  19.9 6.3 %collective-permute-start.2 = (bf16[68,4,264]{2,1,0:T(4,128)(2,1)S(1)}, bf16[68,4,264]{2,1,0:T(4,128)(2,1)S(1)}, u32[]{:S(2)}, u32[]{:S(2)}) collective-permute-start(bf16[68,4,264]{2,1,0:T(4,128)(2,1)S(1)} %get-tuple-element.34), channel_id=1, source_target_pairs={{0,2},{2,4},{4,6},{6,8},{8,10},{10,12},{12,14},{1,3},{3,5},{5,7},{... | collective-permute-start | bytes 430856 | tf_op jit(solution)/shard_map/ppermute | solution.py:21
  23.5 6.7 %collective-permute-start.3 = (bf16[68,4,264]{2,1,0:T(4,128)(2,1)S(1)}, bf16[68,4,264]{2,1,0:T(4,128)(2,1)S(1)}, u32[]{:S(2)}, u32[]{:S(2)}) collective-permute-start(bf16[68,4,264]{2,1,0:T(4,128)(2,1)S(1)} %get-tuple-element.35), channel_id=1, source_target_pairs={{2,0},{4,2},{6,4},{8,6},{10,8},{12,10},{14,12},{3,1},{5,3},{7,5},{... | collective-permute-start | bytes 430856 | tf_op jit(solution)/shard_map/ppermute | solution.py:22
  41.2 35.6 %copy-start.1 = (f32[65,16,256]{2,1,0:T(8,128)}, f32[65,16,256]{2,1,0:T(8,128)S(1)}, u32[]{:S(2)}) copy-start(f32[65,16,256]{2,1,0:T(8,128)S(1)} %fusion.56) | copy-start | bytes 3194884
  41.3 1.2 copy-start.7
  42.4 17.0 %copy-start.3 = (s32[16,256]{1,0:T(8,128)S(1)}, s32[16,256]{1,0:T(8,128)}, u32[]{:S(2)}) copy-start(s32[16,256]{1,0:T(8,128)} %param.18) | copy-start | bytes 49156
  42.4 17.1 %copy-start.2 = (bf16[2,64,16,256]{3,2,1,0:T(8,128)(2,1)S(1)}, bf16[2,64,16,256]{3,2,1,0:T(8,128)(2,1)}, u32[]{:S(2)}) copy-start(bf16[2,64,16,256]{3,2,1,0:T(8,128)(2,1)} %param.14) | copy-start | bytes 3145732
  44.7 26.5 %all-to-all-start = ((f32[128,1,384]{2,1,0:T(1,128)}), f32[128,1,384]{2,1,0:T(1,128)S(1)}, u32[]{:S(2)}, u32[]{:S(2)}) async-start(f32[128,1,384]{2,1,0:T(1,128)} %reshape.150), calls=%async_computation | async-start | bytes 393216 | tf_op jit(solution)/shard_map/all_to_all | solution.py:30
  59.4 93.5 %all-gather.3.cloned.1.call-start = ((), (), s32[]{:S(2)}) async-start(), calls=%async_computation.1 | async-start | bytes 4718592 | tf_op jit(solution)/shard_map/all_gather | solution.py:193
  73.9 3.1 %copy-start = (bf16[8,8,16,256]{3,1,2,0:T(8,128)(2,1)S(1)}, bf16[8,8,16,256]{3,1,2,0:T(8,128)(2,1)}, u32[]{:S(2)}) copy-start(bf16[8,8,16,256]{3,1,2,0:T(8,128)(2,1)} %copy.84) | copy-start | bytes 1572868
  159.4 2.1 %slice-start = ((f32[65,16,256]{2,1,0:T(8,128)}), f32[1,16,256]{2,1,0:T(8,128)S(1)}, s32[]{:S(2)}) async-start(f32[65,16,256]{2,1,0:T(8,128)} %copy-done.1), calls=%async_computation.3 | async-start | bytes 32768 | tf_op jit(solution)/shard_map/slice | solution.py:124
  159.4 2.1 %copy-start.4 = (f32[2,16,256]{2,1,0:T(8,128)S(1)}, f32[2,16,256]{2,1,0:T(8,128)}, u32[]{:S(2)}) copy-start(f32[2,16,256]{2,1,0:T(8,128)} %param.15) | copy-start | bytes 98308
Sparse Core Ops, SparseCore 0:
  42.5 19.9 all-gather.4
  64.9 20.6 all-gather.2
where the time goes:
time: 170 us; the launch traced here: 169 us
  blocking collectives  65.6 us (39%)
  starting transfers between devices  25.7 us (15%)
  other arithmetic  18.3 us (11%)
  local copies, waits for them, and re-layouts  15.7 us (9%)
  between operations  15.4 us (9%)
  matrix products  14.5 us (9%)
  waiting for transfers between devices  13.7 us (8%)
    psum x3, blocking collectives, over_axes(): x = lax.psum(x, axis)  44.5 us
    all_gather x1, blocking collectives, side_by_side(): out = lax.all_gather(both, axis, axis=dim, tiled=True)  21.1 us
    all_to_all x1, starting transfers between devices, sent_together(): lax.all_to_all(both, axis, split_axis=split_dim, concat_axis=concat_dim,...  14.7 us
    sub x4, other arithmetic, upwind(): return center - wet_mask * tendency  8.92 us
    all_to_all x1, waiting for transfers between devices, sent_together(): lax.all_to_all(both, axis, split_axis=split_dim, concat_axis=concat_dim,...  7.95 us
    unnamed x30, local copies, waits for them, and re-layouts  5.93 us
    ppermute x2, starting transfers between devices, with_halo(): before = lax.ppermute(last, axis, up)  5.65 us
    ppermute x2, starting transfers between devices, with_halo(): after = lax.ppermute(leading, axis, down)  5.26 us
  transfers between devices with their start and end apart: 7, of which 4 were waited for; matrix products, arithmetic and copies ran while one was open for 13% of the time, Pallas kernels for 0%

commit v1 on v0

--- a/solution.py
+++ b/solution.py
@@ -33,7 +33,11 @@
 
 def over_axes(x, axes):
     for axis in axes:
-        x = lax.psum(x, axis)
+
+        def draw_case_all(local_block):
+            return lax.all_gather(local_block, axis).sum(axis=0)
+
+        x = draw_case_all(x)
     return x
 
 

time: 170 us -> 193 us (1.14)
  blocking collectives: 65.6 us -> 88 us
  waiting for transfers between devices: 13.7 us -> 10 us
  local copies, waits for them, and re-layouts: 15.7 us -> 18.4 us
  between operations: 15.4 us -> 17.4 us
    psum x3 -> x0, blocking collectives: 44.5 us -> none  [over_axes(): x = lax.psum(x, axis)]
    all_gather x0 -> x3, blocking collectives: none -> 37.3 us  [draw_case_all(): return lax.all_gather(local_block, axis).sum(axis=0)]
    unnamed x0 -> x3, blocking collectives: none -> 25.9 us
    all_gather x1, blocking collectives: 21.1 us -> 24.8 us  [side_by_side(): out = lax.all_gather(both, axis, axis=dim, tiled=True)]
    all_to_all x1, waiting for transfers between devices: 7.95 us -> 4.25 us  [sent_together(): lax.all_to_all(both, axis, split_axis=split_dim, concat_axis=concat_dim,...]
    unnamed x30 -> x46, local copies, waits for them, and re-layouts: 5.93 us -> 8.48 us
where the time goes in v1:
time: 193 us
  blocking collectives  88 us (46%)
  starting transfers between devices  25.7 us (13%)
  local copies, waits for them, and re-layouts  18.4 us (10%)
  other arithmetic  18.4 us (10%)
  between operations  17.4 us (9%)
  matrix products  14.5 us (8%)
  waiting for transfers between devices  10 us (5%)
    all_gather x3, blocking collectives, draw_case_all(): return lax.all_gather(local_block, axis).sum(axis=0)  37.3 us
    unnamed x3, blocking collectives  25.9 us
    all_gather x1, blocking collectives, side_by_side(): out = lax.all_gather(both, axis, axis=dim, tiled=True)  24.8 us
    all_to_all x1, starting transfers between devices, sent_together(): lax.all_to_all(both, axis, split_axis=split_dim, concat_axis=concat_dim,...  14.7 us
    sub x4, other arithmetic, upwind(): return center - wet_mask * tendency  8.92 us
    unnamed x46, local copies, waits for them, and re-layouts  8.48 us
    ppermute x2, starting transfers between devices, with_halo(): before = lax.ppermute(last, axis, up)  5.65 us
    ppermute x2, starting transfers between devices, with_halo(): after = lax.ppermute(leading, axis, down)  5.26 us
  transfers between devices with their start and end apart: 7, of which 4 were waited for; matrix products, arithmetic and copies ran while one was open for 13% of the time, Pallas kernels for 0%

profile of v1, /device:TPU:1, one launch (start us, length us, event | category | flops | bytes accessed | tf_op | source)
XLA Modules:
  0.0 192.5 jit_solution(17746795382664871909)
XLA Ops:
  7.3 1.1 convert_dynamic-update-slice_fusion
  8.3 0.7 bitcast_dynamic-update-slice_fusion.3
  9.1 0.7 bitcast_dynamic-update-slice_fusion.2
  9.8 0.7 bitcast_dynamic-update-slice_fusion.1
  10.5 0.7 bitcast_dynamic-update-slice_fusion
  11.4 0.3 copy.68
  11.7 2.1 %collective-permute-start = (bf16[68,16,4]{0,1,2:T(8,128)(2,1)S(1)}, bf16[68,16,4]{0,1,2:T(8,128)(2,1)S(1)}, u32[]{:S(2)}, u32[]{:S(2)}) collective-permute-start(bf16[68,16,4]{0,1,2:T(8,128)(2,1)S(1)} %copy.68), channel_id=1, source_target_pairs={{0,16},{16,32},{32,48},{48,64},{64,80},{80,96},{96,112},{112,128},... | collective-permute-start | bytes 26120 | tf_op jit(solution)/shard_map/ppermute | solution.py:21
  13.8 0.3 copy.69
  14.1 3.8 %collective-permute-start.1 = (bf16[68,16,4]{0,1,2:T(8,128)(2,1)S(1)}, bf16[68,16,4]{0,1,2:T(8,128)(2,1)S(1)}, u32[]{:S(2)}, u32[]{:S(2)}) collective-permute-start(bf16[68,16,4]{0,1,2:T(8,128)(2,1)S(1)} %copy.69), channel_id=1, source_target_pairs={{16,0},{32,16},{48,32},{64,48},{80,64},{96,80},{112,96},{128,112},... | collective-permute-start | bytes 26120 | tf_op jit(solution)/shard_map/ppermute | solution.py:22
  18.1 0.5 collective-permute-done
  18.6 0.3 copy.70
  19.0 0.3 copy.71
  19.3 0.6 pad_maximum_fusion.4
  19.9 3.6 %collective-permute-start.2 = (bf16[68,4,264]{2,1,0:T(4,128)(2,1)S(1)}, bf16[68,4,264]{2,1,0:T(4,128)(2,1)S(1)}, u32[]{:S(2)}, u32[]{:S(2)}) collective-permute-start(bf16[68,4,264]{2,1,0:T(4,128)(2,1)S(1)} %get-tuple-element.28), channel_id=1, source_target_pairs={{0,2},{2,4},{4,6},{6,8},{8,10},{10,12},{12,14},{1,3},{3,5},{5,7},{... | collective-permute-start | bytes 430856 | tf_op jit(solution)/shard_map/ppermute | solution.py:21
  23.5 1.5 collective-permute-start.3
  24.9 1.2 collective-permute-done.2
  26.2 4.0 %collective-permute-done.3 = bf16[68,4,264]{2,1,0:T(4,128)(2,1)S(1)} collective-permute-done((bf16[68,4,264]{2,1,0:T(4,128)(2,1)S(1)}, bf16[68,4,264]{2,1,0:T(4,128)(2,1)S(1)}, u32[]{:S(2)}, u32[]{:S(2)}) %collective-permute-start.3) | collective-permute-done | bytes 143648 | tf_op jit(solution)/shard_map/ppermute | solution.py:22
  30.7 1.3 maximum_convert_fusion
  32.0 2.6 %fusion.30 = f32[65,22,262]{2,1,0:T(8,128)S(1)} fusion(f32[68,24,264]{2,1,0:T(8,128)S(1)} %maximum_convert_fusion, f32[22,262]{1,0:T(8,128)S(1)} %get-tuple-element.53, f32[22,262]{1,0:T(8,128)S(1)} %get-tuple-element.26, f32[22,262]{1,0:T(8,128)S(1)} %get-tuple-element.52, f32[22,262]{1,0:T(8,128)S(1)} %get-tuple-element.16, ...), kind=kLoop, calls=%fused_computation.41 | loop fusion | flops 4870580 | bytes 9107120 | tf_op jit(solution)/shard_map/sub | solution.py:61
  34.7 2.6 %fusion.21 = f32[65,20,260]{2,1,0:T(8,128)S(1)} fusion(f32[65,22,262]{2,1,0:T(8,128)S(1)} %fusion.30, f32[20,260]{1,0:T(8,128)S(1)} %get-tuple-element.55, f32[20,260]{1,0:T(8,128)S(1)} %get-tuple-element.24, f32[20,260]{1,0:T(8,128)S(1)} %get-tuple-element.54, f32[20,260]{1,0:T(8,128)S(1)} %get-tuple-element.12, f32[20,260]{1,0:T(8,128)S(1)} %convert_bitcast_fusion.1), kind=kLoop, calls=%fused_computation.28 | loop fusion | flops 4394000 | bytes 8216000 | tf_op jit(solution)/shard_map/sub | solution.py:61
  37.4 2.6 %fusion.12 = f32[65,18,258]{2,1,0:T(8,128)S(1)} fusion(f32[65,20,260]{2,1,0:T(8,128)S(1)} %fusion.21, f32[18,258]{1,0:T(8,128)S(1)} %get-tuple-element.57, f32[18,258]{1,0:T(8,128)S(1)} %get-tuple-element.22, f32[18,258]{1,0:T(8,128)S(1)} %get-tuple-element.56, f32[18,258]{1,0:T(8,128)S(1)} %get-tuple-element.8, f32[18,258]{1,0:T(8,128)S(1)} %convert_bitcast_fusion), kind=kLoop, calls=%fused_computation.15 | loop fusion | flops 3924180 | bytes 7337520 | tf_op jit(solution)/shard_map/sub | solution.py:61
  40.1 1.2 fusion.56
  41.3 1.1 copy.87
  42.5 0.4 fusion.69
  43.1 0.3 fusion.118
  43.3 0.4 pad_maximum_fusion.1
  43.8 0.9 reshape.171
  44.7 14.7 %all-to-all-start = ((f32[128,1,384]{2,1,0:T(1,128)}), f32[128,1,384]{2,1,0:T(1,128)S(1)}, u32[]{:S(2)}, u32[]{:S(2)}) async-start(f32[128,1,384]{2,1,0:T(1,128)} %reshape.171), calls=%async_computation | async-start | bytes 393216 | tf_op jit(solution)/shard_map/all_to_all | solution.py:30
  59.5 0.6 dynamic-slice
  60.1 0.6 dynamic-slice.1
  61.9 0.6 dynamic-slice.2
  63.2 1.3 concatenate.39
  64.5 1.1 concatenate.38
  65.7 1.3 pad_maximum_fusion
  67.0 4.3 %all-to-all-done = f32[128,1,384]{2,1,0:T(1,128)S(1)} async-done(((f32[128,1,384]{2,1,0:T(1,128)}), f32[128,1,384]{2,1,0:T(1,128)S(1)}, u32[]{:S(2)}, u32[]{:S(2)}) %all-to-all-start) | async-done | bytes 196640 | tf_op jit(solution)/shard_map/all_to_all | solution.py:30
  71.2 0.5 broadcast.168
  71.7 1.1 reduce.2
  73.6 0.3 fusion.65
  74.0 3.0 %fusion = f32[64,256]{1,0:T(8,128)S(1)} fusion(s32[16384]{0:T(1024)S(1)} %get-tuple-element.49, bf16[16,16384]{1,0:T(8,128)(2,1)S(1)} %get-tuple-element.43, bf16[16,16384]{1,0:T(8,128)(2,1)S(1)} %get-tuple-element.44, bf16[16,16384]{1,0:T(8,128)(2,1)S(1)} %get-tuple-element.45, bf16[16,16384]{1,0:T(8,128)(2,1)S(1)} %get-tuple-element.42), kind=kOutput, calls=%fused_computation.1 | convolution fusion | flops 549453824 | bytes 2228224 | tf_op jit(solution)/shard_map/dot_general | solution.py:165
  77.0 0.2 convolution_bitcast_fusion.3
  77.5 6.3 %all-reduce = f32[256]{0:T(256)S(1)} all-reduce(f32[256]{0:T(256)S(1)} %dynamic-update-slice), channel_id=5, replica_groups=mesh['lon_0'=4,'lon_1'=4,'lat'=8,'mem'=2] {'lon_0'}, use_global_device_ids=true, to_apply=%add | all-reduce | flops 256 | bytes 2048
  83.8 0.2 dynamic-update-slice.1
  84.1 6.8 %all-reduce.1 = f32[256]{0:T(256)S(1)} all-reduce(f32[256]{0:T(256)S(1)} %dynamic-update-slice.1), channel_id=6, replica_groups=mesh['lon_0'=4,'lon_1'=4,'lat'=8,'mem'=2] {'lon_1'}, use_global_device_ids=true, to_apply=%add.1 | all-reduce | flops 256 | bytes 2048
  90.9 0.2 dynamic-update-slice.2
  91.2 12.9 %all-reduce.2 = f32[512]{0:T(512)S(1)} all-reduce(f32[512]{0:T(512)S(1)} %dynamic-update-slice.2), channel_id=7, replica_groups=mesh['lon_0'=4,'lon_1'=4,'lat'=8,'mem'=2] {'lat'}, use_global_device_ids=true, to_apply=%add.2 | all-reduce | flops 512 | bytes 4096
  104.3 1.7 fusion.66
  106.0 9.1 %all-gather = f32[256,128]{1,0:T(8,128)S(1)} all-gather(f32[64,128]{1,0:T(8,128)S(1)} %fusion.66), channel_id=2, replica_groups=mesh['lon_0'=4,'lon_1'=4,'lat'=8,'mem'=2] {'lon_0'}, dimensions={0}, use_global_device_ids=true | all-gather | bytes 163840 | tf_op jit(solution)/shard_map/all_gather | solution.py:38
  115.2 9.1 %all-gather.1 = f32[256,128]{1,0:T(8,128)S(1)} all-gather(f32[64,128]{1,0:T(8,128)S(1)} %reduce_sum.76), channel_id=3, replica_groups=mesh['lon_0'=4,'lon_1'=4,'lat'=8,'mem'=2] {'lon_1'}, dimensions={0}, use_global_device_ids=true | all-gather | bytes 163840 | tf_op jit(solution)/shard_map/all_gather | solution.py:38
  124.3 19.0 %all-gather.2 = f32[512,128]{1,0:T(8,128)S(1)} all-gather(f32[64,128]{1,0:T(8,128)S(1)} %reduce_sum.77), channel_id=4, replica_groups=mesh['lon_0'=4,'lon_1'=4,'lat'=8,'mem'=2] {'lat'}, dimensions={0}, use_global_device_ids=true | all-gather | bytes 294912 | tf_op jit(solution)/shard_map/all_gather | solution.py:38
  143.3 24.8 %all_gather.59 = f32[128,129]{1,0:T(8,128)S(1)} all-gather(f32[64,129]{1,0:T(8,128)S(1)} %pad_maximum_fusion.5), channel_id=1, replica_groups=mesh['lon_0'=4,'lon_1'=4,'lat'=8,'mem'=2] {'mem'}, dimensions={0}, use_global_device_ids=true | all-gather | bytes 99072 | tf_op jit(solution)/shard_map/all_gather | solution.py:49
  168.4 0.6 reduce_max.9
  169.0 0.8 fusion.50
  169.8 0.9 fusion.96
  170.9 0.2 fusion.49
  171.5 0.2 fusion.48
  172.2 0.2 fusion.47
  173.6 0.2 fusion.46
  175.5 0.2 fusion.43
  175.7 0.3 convolution_divide_fusion
  176.4 4.2 %reshape.129 = bf16[3,128,4096]{2,1,0:T(8,128)(2,1)S(1)} reshape(bf16[3,128,16,256]{3,2,1,0:T(8,128)(2,1)} %all-gather.9.cloned.1.call-done) | data formatting | bytes 6291456 | tf_op jit(solution)/shard_map/reshape | solution.py:199
  180.6 2.3 %fusion.5 = bf16[3,64,4096]{2,1,0:T(8,128)(2,1)S(1)} fusion(bf16[3,128,4096]{2,1,0:T(8,128)(2,1)S(1)} %reshape.129, bf16[2,64,4096]{2,1,0:T(8,128)(2,1)} %concatenate.39, bf16[1,64,4096]{2,1,0:T(8,128)(2,1)} %concatenate.38, f32[4096]{0:T(1024)S(1)} %bitcast.219, f32[128,128]{0,1:T(8,128)S(1)} %convolution_divide_fusion, s32[]{:T(128)S(6)} %select_n.47), kind=kOutput, calls=%fused_computation.7 | convolution fusion | flops 206061568 | bytes 6340612 | tf_op jit(solution)/shard_map/nk,snc->skc/dot_general | solution.py:200
  182.9 1.6 copy.90
  184.5 0.5 fusion.6
  185.0 0.6 maximum_add_fusion
  (103 shorter events, 6.7 us)
Async XLA Ops:
  7.2 10.8 %copy-start.5 = (f32[128,64]{0,1:T(8,128)S(1)}, f32[128,64]{0,1:T(8,128)}, u32[]{:S(2)}) copy-start(f32[128,64]{0,1:T(8,128)} %param.20) | copy-start | bytes 98308
  7.2 10.7 %copy-start.8 = (s32[128]{0:T(128)S(1)}, s32[128]{0:T(128)}, u32[]{:S(2)}) copy-start(s32[128]{0:T(128)} %param.23) | copy-start | bytes 1540
  7.2 10.8 %copy-start.9 = (s32[128,1]{0,1:T(1,128)S(1)}, s32[128,1]{0,1:T(1,128)}, u32[]{:S(2)}) copy-start(s32[128,1]{0,1:T(1,128)} %param.22) | copy-start | bytes 1540
  7.2 10.9 %copy-start.6 = (s32[128,64]{0,1:T(8,128)S(1)}, s32[128,64]{0,1:T(8,128)}, u32[]{:S(2)}) copy-start(s32[128,64]{0,1:T(8,128)} %param.21) | copy-start | bytes 98308
  7.2 97.1 %all-gather.11.cloned.1.call-start = ((), (), s32[]{:S(2)}) async-start(), calls=%async_computation.2 | async-start | bytes 1572864 | tf_op jit(solution)/shard_map/all_gather | solution.py:175
  11.7 6.9 %collective-permute-start = (bf16[68,16,4]{0,1,2:T(8,128)(2,1)S(1)}, bf16[68,16,4]{0,1,2:T(8,128)(2,1)S(1)}, u32[]{:S(2)}, u32[]{:S(2)}) collective-permute-start(bf16[68,16,4]{0,1,2:T(8,128)(2,1)S(1)} %copy.68), channel_id=1, source_target_pairs={{0,16},{16,32},{32,48},{48,64},{64,80},{80,96},{96,112},{112,128},... | collective-permute-start | bytes 26120 | tf_op jit(solution)/shard_map/ppermute | solution.py:21
  14.1 4.8 %collective-permute-start.1 = (bf16[68,16,4]{0,1,2:T(8,128)(2,1)S(1)}, bf16[68,16,4]{0,1,2:T(8,128)(2,1)S(1)}, u32[]{:S(2)}, u32[]{:S(2)}) collective-permute-start(bf16[68,16,4]{0,1,2:T(8,128)(2,1)S(1)} %copy.69), channel_id=1, source_target_pairs={{16,0},{32,16},{48,32},{64,48},{80,64},{96,80},{112,96},{128,112},... | collective-permute-start | bytes 26120 | tf_op jit(solution)/shard_map/ppermute | solution.py:22
  19.9 6.3 %collective-permute-start.2 = (bf16[68,4,264]{2,1,0:T(4,128)(2,1)S(1)}, bf16[68,4,264]{2,1,0:T(4,128)(2,1)S(1)}, u32[]{:S(2)}, u32[]{:S(2)}) collective-permute-start(bf16[68,4,264]{2,1,0:T(4,128)(2,1)S(1)} %get-tuple-element.28), channel_id=1, source_target_pairs={{0,2},{2,4},{4,6},{6,8},{8,10},{10,12},{12,14},{1,3},{3,5},{5,7},{... | collective-permute-start | bytes 430856 | tf_op jit(solution)/shard_map/ppermute | solution.py:21
  23.5 6.7 %collective-permute-start.3 = (bf16[68,4,264]{2,1,0:T(4,128)(2,1)S(1)}, bf16[68,4,264]{2,1,0:T(4,128)(2,1)S(1)}, u32[]{:S(2)}, u32[]{:S(2)}) collective-permute-start(bf16[68,4,264]{2,1,0:T(4,128)(2,1)S(1)} %get-tuple-element.29), channel_id=1, source_target_pairs={{2,0},{4,2},{6,4},{8,6},{10,8},{12,10},{14,12},{3,1},{5,3},{7,5},{... | collective-permute-start | bytes 430856 | tf_op jit(solution)/shard_map/ppermute | solution.py:22
  41.2 35.7 %copy-start.1 = (f32[65,16,256]{2,1,0:T(8,128)}, f32[65,16,256]{2,1,0:T(8,128)S(1)}, u32[]{:S(2)}) copy-start(f32[65,16,256]{2,1,0:T(8,128)S(1)} %fusion.56) | copy-start | bytes 3194884
  41.3 1.2 copy-start.7
  42.4 17.0 %copy-start.12 = (u32[256]{0:T(256)S(1)}, u32[256]{0:T(256)}, u32[]{:S(2)}) copy-start(u32[256]{0:T(256)} %constant.63) | copy-start | bytes 3076
  42.4 17.6 %copy-start.11 = (u32[256]{0:T(256)S(1)}, u32[256]{0:T(256)}, u32[]{:S(2)}) copy-start(u32[256]{0:T(256)} %constant.68) | copy-start | bytes 3076
  42.4 19.5 %copy-start.10 = (u32[256]{0:T(256)S(1)}, u32[256]{0:T(256)}, u32[]{:S(2)}) copy-start(u32[256]{0:T(256)} %constant.73) | copy-start | bytes 3076
  42.4 20.8 %copy-start.3 = (s32[16,256]{1,0:T(8,128)S(1)}, s32[16,256]{1,0:T(8,128)}, u32[]{:S(2)}) copy-start(s32[16,256]{1,0:T(8,128)} %param.18) | copy-start | bytes 49156
  42.4 20.8 %copy-start.2 = (bf16[2,64,16,256]{3,2,1,0:T(8,128)(2,1)S(1)}, bf16[2,64,16,256]{3,2,1,0:T(8,128)(2,1)}, u32[]{:S(2)}) copy-start(bf16[2,64,16,256]{3,2,1,0:T(8,128)(2,1)} %param.14) | copy-start | bytes 3145732
  44.7 26.5 %all-to-all-start = ((f32[128,1,384]{2,1,0:T(1,128)}), f32[128,1,384]{2,1,0:T(1,128)S(1)}, u32[]{:S(2)}, u32[]{:S(2)}) async-start(f32[128,1,384]{2,1,0:T(1,128)} %reshape.171), calls=%async_computation | async-start | bytes 393216 | tf_op jit(solution)/shard_map/all_to_all | solution.py:30
  59.4 117.0 %all-gather.9.cloned.1.call-start = ((), (), s32[]{:S(2)}) async-start(), calls=%async_computation.1 | async-start | bytes 4718592 | tf_op jit(solution)/shard_map/all_gather | solution.py:197
  74.0 3.1 %copy-start = (bf16[8,8,16,256]{3,1,2,0:T(8,128)(2,1)S(1)}, bf16[8,8,16,256]{3,1,2,0:T(8,128)(2,1)}, u32[]{:S(2)}) copy-start(bf16[8,8,16,256]{3,1,2,0:T(8,128)(2,1)} %copy.87) | copy-start | bytes 1572868
  182.9 2.1 %slice-start = ((f32[65,16,256]{2,1,0:T(8,128)}), f32[1,16,256]{2,1,0:T(8,128)S(1)}, s32[]{:S(2)}) async-start(f32[65,16,256]{2,1,0:T(8,128)} %copy-done.1), calls=%async_computation.3 | async-start | bytes 32768 | tf_op jit(solution)/shard_map/slice | solution.py:128
  182.9 2.1 %copy-start.4 = (f32[2,16,256]{2,1,0:T(8,128)S(1)}, f32[2,16,256]{2,1,0:T(8,128)}, u32[]{:S(2)}) copy-start(f32[2,16,256]{2,1,0:T(8,128)} %param.15) | copy-start | bytes 98308
Sparse Core Ops, SparseCore 0:
  42.6 19.9 all-gather.10
  67.1 22.2 all-gather.8
